TPU v7x, 32 devices: a whole 2x2x4 slice. The times are simulated.
32 devices in a mesh: groups: 2 (over x), blk: 4 (over y, core), ref: 4 (over z).
Axes of the slice: x: 2, y: 2, z: 4, core: 2. Of those that a mesh axis runs over, the one named last changes fastest.
Arguments:
- queries: bfloat16 [4096, 1024], P(('groups', 'blk')), parts along dimension 0, may hold values from -4 to 4
- references: bfloat16 [8192, 1024], P(('groups', 'blk', 'ref')), parts along dimension 0, may hold values from -4 to 4
- labels: bfloat16 [8192, 512], P(('groups', 'blk', 'ref')), parts along dimension 0, may hold values from 0.0009994507 to 1
Outputs:
- log_scores: float32 [4096, 512], P(('groups', 'blk', 'ref')), parts along dimension 0
There are 2 independent parts, one for each index of `groups`. A program takes and returns all parts, laid end to end along the dimension named above; each array names one. Nothing has to cross between parts.
All inputs are finite; a program needn't handle non-finite values.
Results may differ from a plain program's by a relative error of at most 0.007.
Values may be sent and summed in bfloat16 or wider, within the bound.
No kernel may reach another device: no remote copies, remote signals or barrier semaphores. Data moves between devices by JAX's collectives and lax.ppermute only.
A program may use at most 128 MiB of HBM per device.

v0:
```python
import math
import jax
import jax.numpy as jnp
from jax import lax
from jax.sharding import PartitionSpec as P

NEG_FLOOR = -1e30


def merged(value, axis, join):
    pieces = jax.tree.map(lambda part: lax.all_gather(part, axis), value)
    head = jax.tree.map(lambda part: part[0], pieces)
    tail = jax.tree.map(lambda part: part[1:], pieces)
    subtotal, _ = lax.scan(lambda subtotal, piece: (join(subtotal, piece), None), head, tail)
    return subtotal


def absorb(running, queries, ref_rows, label_rows, score_scale):
    row_top, row_total, row_mass = running
    scores = (
        lax.dot_general(
            queries, ref_rows, (((1,), (1,)), ((), ())), preferred_element_type=jnp.float32
        )
        * score_scale
    )
    new_top = jnp.maximum(row_top, jnp.max(scores, axis=1))
    shrink = jnp.exp(row_top - new_top)
    weights = jnp.exp(scores - new_top[:, None]).astype(jnp.bfloat16)
    row_total = row_total * shrink + jnp.sum(weights.astype(jnp.float32), axis=1)
    row_mass = row_mass * shrink[:, None] + jnp.dot(
        weights, label_rows, preferred_element_type=jnp.float32
    )
    return (new_top, row_total, row_mass)


def combine(first, second):
    new_top = jnp.maximum(first[0], second[0])
    scale_first = jnp.exp(first[0] - new_top)
    scale_second = jnp.exp(second[0] - new_top)
    row_total = first[1] * scale_first + second[1] * scale_second
    row_mass = first[2] * scale_first[:, None] + second[2] * scale_second[:, None]
    return (new_top, row_total, row_mass)


def per_device(queries, references, labels):
    width = queries.shape[1]
    classes = labels.shape[1]
    query_rows = queries.shape[0]
    score_scale = 2.0 / math.sqrt(width)
    initial = (
        jnp.full((query_rows,), NEG_FLOOR, jnp.float32),
        jnp.zeros((query_rows,), jnp.float32),
        jnp.zeros((query_rows, classes), jnp.float32),
    )
    running = initial
    ref_part = lax.all_gather(references, "blk", axis=0, tiled=True)
    label_part = lax.all_gather(labels, "blk", axis=0, tiled=True)
    count = ref_part.shape[0]
    span = math.gcd(count, 512)
    grouped_refs = ref_part.reshape(count // span, span, width)
    grouped_labels = label_part.reshape(count // span, span, classes)

    def advance(current, members):
        return (absorb(current, queries, members[0], members[1], score_scale), None)

    running, unused = lax.scan(advance, running, (grouped_refs, grouped_labels))
    row_top, row_total, row_mass = running
    share = query_rows // lax.axis_size("ref")
    row_top, row_total, row_mass = merged((row_top, row_total, row_mass), "ref", combine)
    offset = lax.axis_index("ref") * share
    mass_rows = lax.dynamic_slice_in_dim(row_mass, offset, share, 0)
    total_rows = lax.dynamic_slice_in_dim(row_total, offset, share, 0)
    return jnp.log(mass_rows) - jnp.log(total_rows)[:, None]


def solution(mesh):
    return jax.shard_map(
        per_device,
        mesh=mesh,
        in_specs=(
            P(("groups", "blk"), None),
            P(("groups", "blk", "ref"), None),
            P(("groups", "blk", "ref"), None),
        ),
        out_specs=P(("groups", "blk", "ref"), None),
        check_vma=False,
    )
```

profile of v0, /device:TPU:0, one launch (start us, length us, event | category | flops | bytes accessed | tf_op | source)
XLA Modules:
  0.0 158.2 jit_solution(7280220137814239432)
XLA Ops:
  6.5 0.0 all-gather.11.cloned.1.call-start
  6.5 0.7 all-gather.11.cloned.1.call-update
  7.3 0.0 all-gather.9.cloned.1.call-start
  7.3 0.7 all-gather.9.cloned.1.call-update
  8.0 0.0 all-gather.13.cloned.1.call-start
  8.1 20.3 %all-gather.11.cloned.1.call-done = bf16[1024,512]{1,0:T(8,128)(2,1)} async-done(((bf16[256,512]{1,0:T(8,128)(2,1)}), bf16[1024,512]{1,0:T(8,128)(2,1)}) %all-gather.11.cloned.1.call-update) | async-done | bytes 1048592 | tf_op jit(solution)/shard_map/all_gather | solution.py:57
  28.3 24.2 %all-gather.9.cloned.1.call-done = bf16[1024,1024]{1,0:T(8,128)(2,1)} async-done(((bf16[256,1024]{1,0:T(8,128)(2,1)}), bf16[1024,1024]{1,0:T(8,128)(2,1)}) %all-gather.9.cloned.1.call-update) | async-done | bytes 2097168 | tf_op jit(solution)/shard_map/all_gather | solution.py:56
  52.5 6.3 %while.30 = (s32[]{:T(128)}, f32[512]{0:T(512)S(1)}, f32[512]{0:T(512)S(1)}, f32[512,512]{1,0:T(8,128)S(1)}, bf16[2,512,1024]{2,1,0:T(8,128)(2,1)}, /*index=5*/b...) while((s32[]{:T(128)}, f32[512]{0:T(512)S(1)}, f32[512]{0:T(512)S(1)}, ...), condition=%wide.region_3.4_spmd.clone, body=%wide.region_0.3_spmd.clone.sunk | while | flops 808192512 | bytes 12092041 | solution.py:66
  52.5 0.0 copy-start.1
  52.5 2.4 %fusion.18 = (f32[512]{0:T(512)S(1)}, f32[512,512]{1,0:T(8,128)S(1)}) fusion(bf16[512,1024]{1,0:T(8,128)(2,1)} %get-tuple-element.278, bf16[2,512,1024]{2,1,0:T(8,128)(2,1)} %get-tuple-element.277, s32[]{:T(128)} %get-tuple-element.264), kind=kOutput, calls=%fused_computation.26.clone.1 | convolution fusion | flops 537394688 | bytes 3148288 | tf_op jit(solution)/shard_map/while/body/eval_jaxpr/dot_general | solution.py:21
  54.9 0.2 convert_reduce_fusion.2
  55.1 0.0 copy-done.1
  55.1 0.5 convolution_add_fusion.2
  55.7 0.0 copy-start.1
  55.7 2.4 %fusion.18 = (f32[512]{0:T(512)S(1)}, f32[512,512]{1,0:T(8,128)S(1)}) fusion(bf16[512,1024]{1,0:T(8,128)(2,1)} %get-tuple-element.278, bf16[2,512,1024]{2,1,0:T(8,128)(2,1)} %get-tuple-element.277, s32[]{:T(128)} %get-tuple-element.264), kind=kOutput, calls=%fused_computation.26.clone.1 | convolution fusion | flops 537394688 | bytes 3148288 | tf_op jit(solution)/shard_map/while/body/eval_jaxpr/dot_general | solution.py:21
  58.1 0.2 convert_reduce_fusion.2
  58.3 0.0 copy-done.1
  58.3 0.5 convolution_add_fusion.2
  58.8 0.0 copy-start
  58.8 1.0 copy-done
  59.8 0.0 all-gather.13.cloned.1.call-update
  59.8 12.0 %all-gather.3 = f32[4,1,512]{2,1,0:T(1,128)S(1)} all-gather(f32[1,1,512]{2,1,0:T(1,128)S(1)} %bitcast.42), channel_id=2, replica_groups=mesh['groups'=2,'blk'=4,'ref'=4] {'ref'}, dimensions={0}, use_global_device_ids=true | all-gather | bytes 10240 | tf_op jit(solution)/shard_map/all_gather | solution.py:11
  71.8 12.4 %all-gather.4 = f32[4,1,512]{2,1,0:T(1,128)S(1)} all-gather(f32[1,1,512]{2,1,0:T(1,128)S(1)} %bitcast.45), channel_id=3, replica_groups=mesh['groups'=2,'blk'=4,'ref'=4] {'ref'}, dimensions={0}, use_global_device_ids=true | all-gather | bytes 10240 | tf_op jit(solution)/shard_map/all_gather | solution.py:11
  84.3 56.6 %all-gather.13.cloned.1.call-done = f32[2048,512]{1,0:T(8,128)} async-done(((f32[512,512]{1,0:T(8,128)}), f32[2048,512]{1,0:T(8,128)}) %all-gather.13.cloned.1.call-update) | async-done | bytes 4194320 | tf_op jit(solution)/shard_map/all_gather | solution.py:11
  140.9 3.9 %slice.39 = f32[1536,512]{1,0:T(8,128)} slice(f32[2048,512]{1,0:T(8,128)} %all-gather.13.cloned.1.call-done), slice={[512:2048], [0:512]} | slice | bytes 6291456 | tf_op jit(solution)/shard_map/slice | solution.py:13
  144.7 1.3 slice.36
  146.0 4.7 %while.29 = (s32[]{:T(128)}, f32[512]{0:T(512)S(1)}, f32[512]{0:T(512)S(1)}, f32[512,512]{1,0:T(8,128)S(1)}, f32[3,512]{1,0:T(4,128)S(1)}, /*index=5*/f32[3,512]{1,0:T(4,128)S(1)}, f32[3,512,512]{2,1,0:T(8,128)}, s32[]{:T(128)}) while((s32[]{:T(128)}, f32[512]{0:T(512)S(1)}, f32[512]{0:T(512)S(1)}, f32[512,512]{1,0:T(8,128)S(1)}, ...), condition=%wide.region_5.6_spmd, body=%wide.region_4.5_spmd.sunk | while | flops 789506 | bytes 3174493 | solution.py:14
  146.1 1.5 fusion.15
  147.6 1.5 fusion.15
  149.2 1.5 fusion.15
  150.8 0.1 dynamic-slice_log_fusion
  150.8 0.8 log_subtract_fusion
  (21 shorter events, 0.2 us)
Async XLA Ops:
  6.5 21.8 %all-gather.11.cloned.1.call-start = ((), (), s32[]{:S(2)}) async-start(), calls=%async_computation.1 | async-start | bytes 1310720 | tf_op jit(solution)/shard_map/all_gather | solution.py:57
  7.3 45.2 %all-gather.9.cloned.1.call-start = ((), (), s32[]{:S(2)}) async-start(), calls=%async_computation | async-start | bytes 2621440 | tf_op jit(solution)/shard_map/all_gather | solution.py:56
  8.0 132.8 %all-gather.13.cloned.1.call-start = ((), (), s32[]{:S(2)}) async-start(), calls=%async_computation.2 | async-start | bytes 5242880 | tf_op jit(solution)/shard_map/all_gather | solution.py:11
  52.5 2.6 %copy-start.1 = (bf16[2,512,512]{2,1,0:T(8,128)(2,1)S(1)}, bf16[2,512,512]{2,1,0:T(8,128)(2,1)}, u32[]{:S(2)}) copy-start(bf16[2,512,512]{2,1,0:T(8,128)(2,1)} %get-tuple-element.279) | copy-start | bytes 3145732 | tf_op jit(solution)/shard_map/while
  55.7 2.6 %copy-start.1 = (bf16[2,512,512]{2,1,0:T(8,128)(2,1)S(1)}, bf16[2,512,512]{2,1,0:T(8,128)(2,1)}, u32[]{:S(2)}) copy-start(bf16[2,512,512]{2,1,0:T(8,128)(2,1)} %get-tuple-element.279) | copy-start | bytes 3145732 | tf_op jit(solution)/shard_map/while
  58.8 1.0 copy-start
Sparse Core Ops, SparseCore 0:
  8.9 19.4 all-gather.10
  29.9 22.5 all-gather.8
  60.0 80.8 all-gather.12
where the time goes:
time: 159 us; the launch traced here: 158 us
  waiting for transfers between devices  102 us (64%)
  blocking collectives  24.4 us (15%)
  between operations  13.2 us (8%)
  local copies, waits for them, and re-layouts  6.26 us (4%)
  other arithmetic  5.86 us (4%)
  matrix products  5.78 us (4%)
    all_gather x1, waiting for transfers between devices, merged(): pieces = jax.tree.map(lambda part: lax.all_gather(part, axis), value)  56.6 us
    all_gather x2, blocking collectives, merged(): pieces = jax.tree.map(lambda part: lax.all_gather(part, axis), value)  24.4 us
    all_gather x1, waiting for transfers between devices, per_device(): ref_part = lax.all_gather(references, 'blk', axis=0, tiled=True)  24.2 us
    all_gather x1, waiting for transfers between devices, per_device(): label_part = lax.all_gather(labels, 'blk', axis=0, tiled=True)  20.3 us
    dot_general x2, matrix products, absorb(): lax.dot_general(queries, ref_rows, (((1,), (1,)), ((), ())), preferred_el...  4.77 us
    add x3, other arithmetic, combine(): first[2] * scale_first[:, None] + second[2] * scale_second[:, None]  4.56 us
    slice x3, local copies, waits for them, and re-layouts, merged(): tail = jax.tree.map(lambda part: part[1:], pieces)  3.87 us
  transfers between devices with their start and end apart: 3, of which 3 were waited for; matrix products, arithmetic and copies ran while one was open for 0% of the time, Pallas kernels for 0%

commit v1 on v0

--- a/solution.py
+++ b/solution.py
@@ -53,7 +53,12 @@
         jnp.zeros((query_rows, classes), jnp.float32),
     )
     running = initial
-    ref_part = lax.all_gather(references, "blk", axis=0, tiled=True)
+    ring = [references]
+    for hop in range(3):
+        ring.append(lax.ppermute(ring[-1], "blk", [(dev, (dev + 1) % 4) for dev in range(4)]))
+    ref_part = jnp.roll(
+        jnp.concatenate(ring[::-1], axis=0), (lax.axis_index("blk") + 1) * ring[0].shape[0], axis=0
+    )
     label_part = lax.all_gather(labels, "blk", axis=0, tiled=True)
     count = ref_part.shape[0]
     span = math.gcd(count, 512)

time: 159 us -> 150 us (0.943)
  waiting for transfers between devices: 102 us -> 90.4 us
  local copies, waits for them, and re-layouts: 6.26 us -> 9.13 us
    ppermute x0 -> x3, waiting for transfers between devices: none -> 26.2 us  [per_device(): lax.ppermute(ring[-1], 'blk', [(dev, (dev + 1) % 4) for dev in range(4)])]
    all_gather x1 -> x0, waiting for transfers between devices: 24.2 us -> none  [per_device(): ref_part = lax.all_gather(references, 'blk', axis=0, tiled=True)]
    all_gather x1, waiting for transfers between devices: 20.3 us -> 7.64 us  [per_device(): label_part = lax.all_gather(labels, 'blk', axis=0, tiled=True)]
  transfers between devices with their start and end apart: 3 -> 5, of which waited for: 3 -> 5; matrix products, arithmetic and copies ran while one was open for 0% -> 2% of each run, Pallas kernels for 0% -> 0%
where the time goes in v1:
time: 150 us
  waiting for transfers between devices  90.4 us (60%)
  blocking collectives  24.4 us (16%)
  between operations  13.6 us (9%)
  local copies, waits for them, and re-layouts  9.13 us (6%)
  other arithmetic  5.86 us (4%)
  matrix products  5.78 us (4%)
    all_gather x1, waiting for transfers between devices, merged(): pieces = jax.tree.map(lambda part: lax.all_gather(part, axis), value)  56.6 us
    ppermute x3, waiting for transfers between devices, per_device(): lax.ppermute(ring[-1], 'blk', [(dev, (dev + 1) % 4) for dev in range(4)])  26.2 us
    all_gather x2, blocking collectives, merged(): pieces = jax.tree.map(lambda part: lax.all_gather(part, axis), value)  24.4 us
    all_gather x1, waiting for transfers between devices, per_device(): label_part = lax.all_gather(labels, 'blk', axis=0, tiled=True)  7.64 us
    dot_general x2, matrix products, absorb(): lax.dot_general(queries, ref_rows, (((1,), (1,)), ((), ())), preferred_el...  4.77 us
    add x3, other arithmetic, combine(): first[2] * scale_first[:, None] + second[2] * scale_second[:, None]  4.56 us
    slice x3, local copies, waits for them, and re-layouts, merged(): tail = jax.tree.map(lambda part: part[1:], pieces)  3.88 us
  transfers between devices with their start and end apart: 5, of which 5 were waited for; matrix products, arithmetic and copies ran while one was open for 2% of the time, Pallas kernels for 0%

profile of v1, /device:TPU:0, one launch (start us, length us, event | category | flops | bytes accessed | tf_op | source)
XLA Modules:
  0.0 149.9 jit_solution(9812553646279890392)
XLA Ops:
  6.5 0.0 copy-start.2
  6.5 0.0 all-gather.8.cloned.1.call-start
  6.5 0.5 collective-permute-start
  7.0 9.1 %collective-permute-done = bf16[256,1024]{1,0:T(8,128)(2,1)S(1)} collective-permute-done((bf16[256,1024]{1,0:T(8,128)(2,1)}, bf16[256,1024]{1,0:T(8,128)(2,1)S(1)}, u32[]{:S(2)}, u32[]{:S(2)}) %collective-permute-start) | collective-permute-done | bytes 524320 | tf_op jit(solution)/shard_map/ppermute | solution.py:58
  16.1 0.0 collective-permute-start.1
  16.1 8.6 %collective-permute-done.1 = bf16[256,1024]{1,0:T(8,128)(2,1)S(1)} collective-permute-done((bf16[256,1024]{1,0:T(8,128)(2,1)S(1)}, bf16[256,1024]{1,0:T(8,128)(2,1)S(1)}, u32[]{:S(2)}, u32[]{:S(2)}) %collective-permute-start.1) | collective-permute-done | bytes 524320 | tf_op jit(solution)/shard_map/ppermute | solution.py:58
  24.7 0.0 collective-permute-start.2
  24.7 0.0 all-gather.8.cloned.1.call-update
  24.8 0.0 all-gather.10.cloned.1.call-start
  24.9 8.5 %collective-permute-done.2 = bf16[256,1024]{1,0:T(8,128)(2,1)S(1)} collective-permute-done((bf16[256,1024]{1,0:T(8,128)(2,1)S(1)}, bf16[256,1024]{1,0:T(8,128)(2,1)S(1)}, u32[]{:S(2)}, u32[]{:S(2)}) %collective-permute-start.2) | collective-permute-done | bytes 524320 | tf_op jit(solution)/shard_map/ppermute | solution.py:58
  33.5 1.1 constant_dynamic-update-slice_fusion.4
  34.7 0.0 copy-done.2
  34.7 1.5 %constant_dynamic-slice_fusion.2 = bf16[1024,1024]{1,0:T(8,128)(2,1)} fusion(bf16[2048,1024]{1,0:T(8,128)(2,1)S(1)} %constant_dynamic-update-slice_fusion, s32[]{:T(128)S(6)} %select_n.18), kind=kLoop, calls=%fused_computation.34 | loop fusion | bytes 4194308 | tf_op jit(solution)/shard_map/jit(_roll_dynamic)/dynamic_slice | solution.py:59
  36.3 7.6 %all-gather.8.cloned.1.call-done = bf16[1024,512]{1,0:T(8,128)(2,1)} async-done(((bf16[256,512]{1,0:T(8,128)(2,1)}), bf16[1024,512]{1,0:T(8,128)(2,1)}) %all-gather.8.cloned.1.call-update) | async-done | bytes 1048592 | tf_op jit(solution)/shard_map/all_gather | solution.py:62
  43.9 6.3 %while.30 = (s32[]{:T(128)}, f32[512]{0:T(512)S(1)}, f32[512]{0:T(512)S(1)}, f32[512,512]{1,0:T(8,128)S(1)}, bf16[2,512,1024]{2,1,0:T(8,128)(2,1)}, /*index=5*/b...) while((s32[]{:T(128)}, f32[512]{0:T(512)S(1)}, f32[512]{0:T(512)S(1)}, ...), condition=%wide.region_3.4_spmd.clone, body=%wide.region_0.3_spmd.clone.sunk | while | flops 808192512 | bytes 12092041 | solution.py:71
  43.9 0.0 copy-start.1
  43.9 2.4 %fusion.18 = (f32[512]{0:T(512)S(1)}, f32[512,512]{1,0:T(8,128)S(1)}) fusion(bf16[512,1024]{1,0:T(8,128)(2,1)} %get-tuple-element.278, bf16[2,512,1024]{2,1,0:T(8,128)(2,1)} %get-tuple-element.277, s32[]{:T(128)} %get-tuple-element.264), kind=kOutput, calls=%fused_computation.35.clone.1 | convolution fusion | flops 537394688 | bytes 3148288 | tf_op jit(solution)/shard_map/while/body/eval_jaxpr/dot_general | solution.py:21
  46.3 0.2 convert_reduce_fusion.2
  46.5 0.0 copy-done.1
  46.5 0.5 convolution_add_fusion.2
  47.1 0.0 copy-start.1
  47.1 2.4 %fusion.18 = (f32[512]{0:T(512)S(1)}, f32[512,512]{1,0:T(8,128)S(1)}) fusion(bf16[512,1024]{1,0:T(8,128)(2,1)} %get-tuple-element.278, bf16[2,512,1024]{2,1,0:T(8,128)(2,1)} %get-tuple-element.277, s32[]{:T(128)} %get-tuple-element.264), kind=kOutput, calls=%fused_computation.35.clone.1 | convolution fusion | flops 537394688 | bytes 3148288 | tf_op jit(solution)/shard_map/while/body/eval_jaxpr/dot_general | solution.py:21
  49.5 0.2 convert_reduce_fusion.2
  49.7 0.0 copy-done.1
  49.7 0.5 convolution_add_fusion.2
  50.2 0.0 copy-start
  50.2 1.0 copy-done
  51.2 0.0 all-gather.10.cloned.1.call-update
  51.2 12.0 %all-gather.3 = f32[4,1,512]{2,1,0:T(1,128)S(1)} all-gather(f32[1,1,512]{2,1,0:T(1,128)S(1)} %bitcast.43), channel_id=2, replica_groups=mesh['groups'=2,'blk'=4,'ref'=4] {'ref'}, dimensions={0}, use_global_device_ids=true | all-gather | bytes 10240 | tf_op jit(solution)/shard_map/all_gather | solution.py:11
  63.2 12.4 %all-gather.4 = f32[4,1,512]{2,1,0:T(1,128)S(1)} all-gather(f32[1,1,512]{2,1,0:T(1,128)S(1)} %bitcast.46), channel_id=3, replica_groups=mesh['groups'=2,'blk'=4,'ref'=4] {'ref'}, dimensions={0}, use_global_device_ids=true | all-gather | bytes 10240 | tf_op jit(solution)/shard_map/all_gather | solution.py:11
  75.7 56.6 %all-gather.10.cloned.1.call-done = f32[2048,512]{1,0:T(8,128)} async-done(((f32[512,512]{1,0:T(8,128)}), f32[2048,512]{1,0:T(8,128)}) %all-gather.10.cloned.1.call-update) | async-done | bytes 4194320 | tf_op jit(solution)/shard_map/all_gather | solution.py:11
  132.2 3.9 %slice.39 = f32[1536,512]{1,0:T(8,128)} slice(f32[2048,512]{1,0:T(8,128)} %all-gather.10.cloned.1.call-done), slice={[512:2048], [0:512]} | slice | bytes 6291456 | tf_op jit(solution)/shard_map/slice | solution.py:13
  136.1 1.3 slice.36
  137.4 4.7 %while.29 = (s32[]{:T(128)}, f32[512]{0:T(512)S(1)}, f32[512]{0:T(512)S(1)}, f32[512,512]{1,0:T(8,128)S(1)}, f32[3,512]{1,0:T(4,128)S(1)}, /*index=5*/f32[3,512]{1,0:T(4,128)S(1)}, f32[3,512,512]{2,1,0:T(8,128)}, s32[]{:T(128)}) while((s32[]{:T(128)}, f32[512]{0:T(512)S(1)}, f32[512]{0:T(512)S(1)}, f32[512,512]{1,0:T(8,128)S(1)}, ...), condition=%wide.region_5.6_spmd, body=%wide.region_4.5_spmd.sunk | while | flops 789506 | bytes 3174493 | solution.py:14
  137.5 1.5 %fusion.15 = f32[512,512]{1,0:T(8,128)S(1)} fusion(f32[3,512,512]{2,1,0:T(8,128)} %get-tuple-element.304, s32[]{:T(128)} %get-tuple-element.290, f32[512,512]{1,0:T(8,128)S(1)} %get-tuple-element.293, f32[512]{0:T(512)S(1)} %get-tuple-element.242, f32[512]{0:T(512)S(1)} %get-tuple-element.243), kind=kLoop, calls=%fused_computation.1.clone.1 | loop fusion | flops 786432 | bytes 3149828 | tf_op jit(solution)/shard_map/while/body/eval_jaxpr/add | solution.py:41
  139.1 1.5 %fusion.15 = f32[512,512]{1,0:T(8,128)S(1)} fusion(f32[3,512,512]{2,1,0:T(8,128)} %get-tuple-element.304, s32[]{:T(128)} %get-tuple-element.290, f32[512,512]{1,0:T(8,128)S(1)} %get-tuple-element.293, f32[512]{0:T(512)S(1)} %get-tuple-element.242, f32[512]{0:T(512)S(1)} %get-tuple-element.243), kind=kLoop, calls=%fused_computation.1.clone.1 | loop fusion | flops 786432 | bytes 3149828 | tf_op jit(solution)/shard_map/while/body/eval_jaxpr/add | solution.py:41
  140.6 1.5 %fusion.15 = f32[512,512]{1,0:T(8,128)S(1)} fusion(f32[3,512,512]{2,1,0:T(8,128)} %get-tuple-element.304, s32[]{:T(128)} %get-tuple-element.290, f32[512,512]{1,0:T(8,128)S(1)} %get-tuple-element.293, f32[512]{0:T(512)S(1)} %get-tuple-element.242, f32[512]{0:T(512)S(1)} %get-tuple-element.243), kind=kLoop, calls=%fused_computation.1.clone.1 | loop fusion | flops 786432 | bytes 3149828 | tf_op jit(solution)/shard_map/while/body/eval_jaxpr/add | solution.py:41
  142.2 0.1 dynamic-slice_log_fusion
  142.3 0.8 log_subtract_fusion
  (28 shorter events, 0.4 us)
Async XLA Ops:
  6.5 28.2 %copy-start.2 = (bf16[256,1024]{1,0:T(8,128)(2,1)S(1)}, bf16[256,1024]{1,0:T(8,128)(2,1)}, u32[]{:S(2)}) copy-start(bf16[256,1024]{1,0:T(8,128)(2,1)} %param.8) | copy-start | bytes 1572868
  6.5 37.4 %all-gather.8.cloned.1.call-start = ((), (), s32[]{:S(2)}) async-start(), calls=%async_computation | async-start | bytes 1310720 | tf_op jit(solution)/shard_map/all_gather | solution.py:62
  6.5 9.6 %collective-permute-start = (bf16[256,1024]{1,0:T(8,128)(2,1)}, bf16[256,1024]{1,0:T(8,128)(2,1)S(1)}, u32[]{:S(2)}, u32[]{:S(2)}) collective-permute-start(bf16[256,1024]{1,0:T(8,128)(2,1)} %param.8), channel_id=1, source_target_pairs={{0,4},{4,8},{8,12},{12,0},{1,5},{5,9},{9,13},{13,1},{2,6},{6,10},{... | collective-permute-start | bytes 1572872 | tf_op jit(solution)/shard_map/ppermute | solution.py:58
  16.1 8.6 %collective-permute-start.1 = (bf16[256,1024]{1,0:T(8,128)(2,1)S(1)}, bf16[256,1024]{1,0:T(8,128)(2,1)S(1)}, u32[]{:S(2)}, u32[]{:S(2)}) collective-permute-start(bf16[256,1024]{1,0:T(8,128)(2,1)S(1)} %collective-permute-done), channel_id=1, source_target_pairs={{0,4},{4,8},{8,12},{12,0},{1,5},{5,9},{9,13},{13,1},{2,6},{6,10},{... | collective-permute-start | bytes 1572872 | tf_op jit(solution)/shard_map/ppermute | solution.py:58
  24.7 8.6 %collective-permute-start.2 = (bf16[256,1024]{1,0:T(8,128)(2,1)S(1)}, bf16[256,1024]{1,0:T(8,128)(2,1)S(1)}, u32[]{:S(2)}, u32[]{:S(2)}) collective-permute-start(bf16[256,1024]{1,0:T(8,128)(2,1)S(1)} %collective-permute-done.1), channel_id=1, source_target_pairs={{0,4},{4,8},{8,12},{12,0},{1,5},{5,9},{9,13},{13,1},{2,6},{6,10},{... | collective-permute-start | bytes 1572872 | tf_op jit(solution)/shard_map/ppermute | solution.py:58
  24.8 107.5 %all-gather.10.cloned.1.call-start = ((), (), s32[]{:S(2)}) async-start(), calls=%async_computation.1 | async-start | bytes 5242880 | tf_op jit(solution)/shard_map/all_gather | solution.py:11
  43.9 2.6 %copy-start.1 = (bf16[2,512,512]{2,1,0:T(8,128)(2,1)S(1)}, bf16[2,512,512]{2,1,0:T(8,128)(2,1)}, u32[]{:S(2)}) copy-start(bf16[2,512,512]{2,1,0:T(8,128)(2,1)} %get-tuple-element.279) | copy-start | bytes 3145732 | tf_op jit(solution)/shard_map/while
  47.1 2.6 %copy-start.1 = (bf16[2,512,512]{2,1,0:T(8,128)(2,1)S(1)}, bf16[2,512,512]{2,1,0:T(8,128)(2,1)}, u32[]{:S(2)}) copy-start(bf16[2,512,512]{2,1,0:T(8,128)(2,1)} %get-tuple-element.279) | copy-start | bytes 3145732 | tf_op jit(solution)/shard_map/while
  50.2 1.0 copy-start
Sparse Core Ops, SparseCore 0:
  24.9 18.9 all-gather.7
  51.3 80.8 all-gather.9
